TPU v7x, 32 devices: a whole 2x2x4 slice. The times are simulated.
32 devices in a mesh: orient: 16 (over z, y, core), frame: 2 (over x).
Axes of the slice: x: 2, y: 2, z: 4, core: 2. Of those that a mesh axis runs over, the one named last changes fastest.
Arguments:
- log_tomograms: bfloat16 [2048, 4096], P('orient'), may hold values from -3 to 3
- frames: int32 [512, 4096], P('frame'), may hold values from 0 to 15, as said below
- tile_index: int32 [2, 32, 2048], P(None, 'frame', 'orient'), may hold values from 0 to 383
- tile_weight: float32 [2, 32, 2048], P(None, 'frame', 'orient'), may hold values from 0.1 to 1
- prior_volume: float32 [2, 384, 128], P('frame', 'orient'), may hold values from 0.5 to 2
Outputs:
- new_log_tomograms: bfloat16 [2048, 4096], P('orient', 'frame')
- volume: float32 [2, 384, 128], P('frame', 'orient')
- evidence: float32 [512], P('frame')
Inputs may be any that keep to these rules, and one draw needn't show every extreme that they name: `frames`: each frame's counts lie below a level of that frame; the first frame has a pixel with 15 photons. `tile_index`: the tile of an entry counts within the shell group of its pixel block.
All inputs are finite; a program needn't handle non-finite values.
Results may differ from a plain program's by a relative error of at most 0.008.
Values may be sent and summed in bfloat16 or wider, within the bound.
A program may use at most 64 MiB of HBM per device.

v0:
```python
import jax
import jax.numpy as jnp
from jax import lax
from jax.sharding import PartitionSpec as P


def merged(value, axis, join):
    pieces = jax.tree.map(lambda part: lax.all_gather(part, axis), value)
    head = jax.tree.map(lambda part: part[0], pieces)
    tail = jax.tree.map(lambda part: part[1:], pieces)
    so_far, _ = lax.scan(lambda so_far, slab: (join(so_far, slab), None), head, tail)
    return so_far


def combine_stats(first_stats, second_stats):
    joined = jnp.maximum(first_stats[0], second_stats[0])
    summed = first_stats[1] * jnp.exp(first_stats[0] - joined) + second_stats[1] * jnp.exp(
        second_stats[0] - joined
    )
    return (joined, summed)


def on_device(log_tomograms, frames, tile_index, tile_weight, prior_volume):
    rot_rows, pixel_count = log_tomograms.shape
    frame_rows = frames.shape[0]
    group_blocks = tile_index.shape[1]
    tile_rows = prior_volume.shape[1]
    tile_width = prior_volume.shape[2]
    orient_count = lax.axis_size("orient")
    frame_count = lax.axis_size("frame")
    inverse_temp = 64.0 / pixel_count
    counts = frames.astype(jnp.bfloat16)
    column_width = pixel_count // frame_count
    column_start = lax.axis_index("frame") * column_width
    intensity = jnp.exp(log_tomograms.astype(jnp.float32))
    tomo_mass = jnp.sum(intensity, axis=1)
    correlation = jnp.einsum("rp,fp->rf", log_tomograms, counts, preferred_element_type=jnp.float32)
    scores = inverse_temp * (correlation - tomo_mass[:, None])
    local_peak = jnp.max(scores, axis=0)
    local_total = jnp.sum(jnp.exp(scores - local_peak[None, :]), axis=0)
    score_peak, score_total = merged((local_peak, local_total), "orient", combine_stats)
    responsibility = jnp.exp(scores - score_peak[None, :]) / score_total[None, :]
    evidence = score_peak + jnp.log(score_total)
    resp_low = responsibility.astype(jnp.bfloat16)
    denominator = jnp.sum(responsibility, axis=1)
    numerator = jnp.dot(resp_low, counts, preferred_element_type=jnp.float32)
    numer_all, denom_all = (
        lax.psum(numerator.astype(jnp.bfloat16), "frame").astype(jnp.float32),
        lax.psum(denominator.astype(jnp.bfloat16), "frame").astype(jnp.float32),
    )
    numer_mine = lax.dynamic_slice_in_dim(numer_all, column_start, column_width, 1)
    intensity_mine = lax.dynamic_slice_in_dim(intensity, column_start, column_width, 1)
    prior_share = frame_rows * frame_count / (rot_rows * orient_count)
    updated = (numer_mine + prior_share * intensity_mine) / (denom_all[:, None] + prior_share)
    block_values = updated.reshape(rot_rows, group_blocks, tile_width).transpose(1, 0, 2)
    tiles_column = tile_rows * orient_count
    flat_ids = tile_index.reshape(-1)
    contrib = (tile_weight[..., None] * block_values[None]).reshape(-1, tile_width)
    numer_tiles = jax.ops.segment_sum(contrib, flat_ids, num_segments=tiles_column)
    weight_tiles = jax.ops.segment_sum(tile_weight.reshape(-1), flat_ids, num_segments=tiles_column)
    numer_own, weight_own = (
        lax.psum_scatter(numer_tiles, "orient", scatter_dimension=0, tiled=True),
        lax.psum_scatter(weight_tiles, "orient", scatter_dimension=0, tiled=True),
    )
    prior_weight = rot_rows * group_blocks / (4.0 * tile_rows)
    volume_own = (numer_own + prior_weight * prior_volume[0]) / (weight_own[:, None] + prior_weight)
    column = lax.all_gather(volume_own, "orient", axis=0, tiled=True)
    blended_sum = jnp.sum(tile_weight[..., None] * column[tile_index], axis=0)
    blended = blended_sum / jnp.sum(tile_weight, axis=0)[..., None]
    new_log = (
        jnp.log(blended).transpose(1, 0, 2).reshape(rot_rows, column_width).astype(jnp.bfloat16)
    )
    return (new_log, volume_own[None], evidence)


def solution(mesh):
    placed = (
        P("orient", None),
        P("frame", None),
        P(None, "frame", "orient"),
        P(None, "frame", "orient"),
        P("frame", "orient", None),
    )
    return jax.shard_map(
        on_device,
        mesh=mesh,
        in_specs=placed,
        out_specs=(P("orient", "frame"), P("frame", "orient", None), P("frame")),
        check_vma=False,
    )
```

profile of v0, /device:TPU:0, one launch (start us, length us, event | category | flops | bytes accessed | tf_op | source)
XLA Modules:
  0.0 240.4 jit_solution(10948065416326428057)
XLA Ops:
  7.2 0.0 copy-start
  7.2 0.0 all-reduce.4.cloned.1.call-start
  7.2 1.7 fusion.5
  8.9 0.0 copy-done
  8.9 3.1 %fusion.13 = (f32[256]{0:T(256)S(1)}, f32[128,256]{1,0:T(8,128)S(1)}) fusion(f32[128]{0:T(128)S(1)} %get-tuple-element.50, bf16[128,4096]{1,0:T(8,128)(2,1)S(1)} %copy-done, s32[256,4096]{1,0:T(8,128)} %param.8), kind=kOutput, calls=%fused_computation.36 | convolution fusion | flops 269582080 | bytes 5375488 | tf_op jit(solution)/shard_map/rp,fp->rf/dot_general | solution.py:37
  12.0 23.2 %all-gather.3 = f32[16,1,256]{2,1,0:T(1,128)S(1)} all-gather(f32[1,1,256]{2,1,0:T(1,128)S(1)} %bitcast.59), channel_id=3, replica_groups=mesh['orient'=16,'frame'=2] {'orient'}, dimensions={0}, use_global_device_ids=true | all-gather | bytes 17408 | tf_op jit(solution)/shard_map/all_gather | solution.py:8
  35.2 17.4 %all-gather.2 = f32[16,1,256]{2,1,0:T(1,128)S(1)} all-gather(f32[1,1,256]{2,1,0:T(1,128)S(1)} %bitcast.58), channel_id=2, replica_groups=mesh['orient'=16,'frame'=2] {'orient'}, dimensions={0}, use_global_device_ids=true | all-gather | bytes 17408 | tf_op jit(solution)/shard_map/all_gather | solution.py:8
  52.7 0.8 while.12
  53.5 0.0 copy-start.1
  53.5 0.0 copy-start.3
  53.5 0.0 copy-start.5
  53.5 3.7 %convolution_convert_fusion = bf16[128,4096]{1,0:T(8,128)(2,1)} fusion(s32[256,4096]{1,0:T(8,128)} %param.8, f32[128,256]{1,0:T(8,128)S(1)} %get-tuple-element.53, f32[256]{0:T(256)S(1)} %get-tuple-element.32, f32[256]{0:T(256)S(1)} %get-tuple-element.31), kind=kOutput, calls=%fused_computation.6 | convolution fusion | flops 270106624 | bytes 5376000 | tf_op jit(solution)/shard_map/dot_general | solution.py:46
  57.2 0.0 all-reduce.4.cloned.1.call-update
  57.2 0.0 reduce-scatter.4.cloned.1.call-start
  57.3 0.0 copy-done.1
  57.3 0.0 copy-done.3
  57.3 28.8 %scatter_custom_fusion.1 = f32[384]{0:T(512)S(1)} fusion(s32[4096]{0:T(1024)S(1)} %bitcast.56, f32[4096]{0:T(1024)S(1)} %bitcast.45, f32[]{:T(128)} %constant.16.clone.1), kind=kCustom, calls=%fused_computation.32 | custom fusion | flops 4096 | bytes 1540 | tf_op jit(solution)/shard_map/scatter-add | solution.py:60
  86.1 0.0 copy-done.5
  86.1 0.6 dynamic-slice
  87.4 0.1 fusion.9
  87.5 5.1 %psum.15 = bf16[128]{0:T(256)(128)(2,1)S(1)} all-reduce(bf16[128]{0:T(256)(128)(2,1)S(1)} %fusion.9), channel_id=1, replica_groups=mesh['orient'=16,'frame'=2] {'frame'}, use_global_device_ids=true, to_apply=%region_7.8 | all-reduce | flops 128 | bytes 512 | tf_op jit(solution)/shard_map/psum | solution.py:49
  92.6 30.3 %all-reduce.1 = f32[384]{0:T(512)S(1)} all-reduce(f32[384]{0:T(512)S(1)} %scatter_custom_fusion.1), channel_id=5, replica_groups=mesh['orient'=16,'frame'=2] {'orient'}, use_global_device_ids=true, to_apply=%region_11.12.clone | all-reduce | flops 384 | bytes 3072
  123.0 0.6 log_add_fusion
  123.5 0.0 all-reduce.4.cloned.1.call-done
  123.5 1.2 divide_bitcast_fusion
  124.8 0.2 copy.15
  125.0 0.3 copy.10
  125.3 0.0 copy-start.4
  125.3 0.6 bitcast_multiply_fusion
  125.9 23.0 %scatter_custom_fusion = f32[384,128]{1,0:T(8,128)} fusion(s32[4096]{0:T(1024)S(1)} %bitcast.57, f32[4096,128]{1,0:T(8,128)S(1)} %bitcast_multiply_fusion, f32[]{:T(128)} %constant.16.clone.1), kind=kCustom, calls=%fused_computation.21 | custom fusion | flops 524288 | bytes 196612 | tf_op jit(solution)/shard_map/scatter-add | solution.py:59
  148.9 0.0 reduce-scatter.4.cloned.1.call-update
  148.9 0.1 dynamic-slice_add_fusion
  149.0 50.6 %reduce-scatter.4.cloned.1.call-done = f32[24,128]{1,0:T(8,128)} async-done(((f32[384,128]{1,0:T(8,128)}), f32[24,128]{1,0:T(8,128)}) %reduce-scatter.4.cloned.1.call-update) | async-done | bytes 12304
  199.6 0.0 copy-done.4
  199.6 0.8 fusion.10
  200.4 0.0 copy-start.2
  200.4 20.0 %all_gather.19 = f32[384,128]{1,0:T(8,128)S(1)} all-gather(f32[24,128]{1,0:T(8,128)S(1)} %fusion.10), channel_id=1, replica_groups=mesh['orient'=16,'frame'=2] {'orient'}, dimensions={0}, use_global_device_ids=true | all-gather | bytes 208896 | tf_op jit(solution)/shard_map/all_gather | solution.py:67
  220.3 10.8 %gather_fusion = f32[4096,128]{1,0:T(8,128)S(1)} fusion(f32[384,128]{1,0:T(8,128)S(1)} %all_gather.19, s32[4096]{0:T(1024)S(1)} %broadcast_clamp_fusion), kind=kCustom, calls=%fused_computation | custom fusion | bytes 4210688 | tf_op jit(solution)/shard_map/gather | solution.py:68
  231.1 0.0 copy-done.2
  231.2 0.8 multiply_reduce_fusion
  231.9 0.3 fusion.2
  232.3 0.3 copy.11
  232.6 1.0 copy.12
  (41 shorter events, 0.5 us)
Async XLA Ops:
  7.2 1.7 copy-start
  7.2 116.4 %all-reduce.4.cloned.1.call-start = ((), (), s32[]{:S(2)}) async-start(), calls=%async_computation.1 | async-start | bytes 2097152 | tf_op jit(solution)/shard_map/psum | solution.py:48
  53.5 3.8 %copy-start.1 = (f32[2,16,128]{2,1,0:T(8,128)S(1)}, f32[2,16,128]{2,1,0:T(8,128)}, u32[]{:S(2)}) copy-start(f32[2,16,128]{2,1,0:T(8,128)} %param.10) | copy-start | bytes 49156
  53.5 3.9 %copy-start.3 = (s32[2,16,128]{2,1,0:T(8,128)S(1)}, s32[2,16,128]{2,1,0:T(8,128)}, u32[]{:S(2)}) copy-start(s32[2,16,128]{2,1,0:T(8,128)} %param.9) | copy-start | bytes 49156
  53.5 32.6 %copy-start.5 = (u32[32]{0:T(128)S(1)}, u32[32]{0:T(128)}, u32[]{:S(2)}) copy-start(u32[32]{0:T(128)} %constant.38) | copy-start | bytes 388
  57.2 142.4 %reduce-scatter.4.cloned.1.call-start = ((), (), s32[]{:S(2)}) async-start(), calls=%async_computation.2 | async-start | bytes 208896
  125.3 74.3 %copy-start.4 = (f32[1,24,128]{2,1,0:T(8,128)S(1)}, f32[1,24,128]{2,1,0:T(8,128)}, u32[]{:S(2)}) copy-start(f32[1,24,128]{2,1,0:T(8,128)} %param.11) | copy-start | bytes 36868
  200.4 30.8 %copy-start.2 = (f32[24,128]{1,0:T(8,128)}, f32[24,128]{1,0:T(8,128)S(1)}, u32[]{:S(2)}) copy-start(f32[24,128]{1,0:T(8,128)S(1)} %fusion.10) | copy-start | bytes 36868
Sparse Core Ops, SparseCore 0:
  57.4 38.5 all-reduce.3
  149.1 50.4 reduce-scatter.3
where the time goes:
time: 241 us; the launch traced here: 240 us
  blocking collectives  96.1 us (40%)
  other arithmetic  58.3 us (24%)
  waiting for transfers between devices  50.6 us (21%)
  between operations  14.9 us (6%)
  local copies, waits for them, and re-layouts  13.4 us (6%)
  matrix products  6.79 us (3%)
    unnamed x3, waiting for transfers between devices  50.6 us
    all_gather x2, blocking collectives, merged(): pieces = jax.tree.map(lambda part: lax.all_gather(part, axis), value)  40.6 us
    unnamed x1, blocking collectives  30.3 us
    scatter-add x1, other arithmetic, on_device(): jax.ops.segment_sum(tile_weight.reshape(-1), flat_ids, num_segments=tiles...  28.8 us
    scatter-add x1, other arithmetic, on_device(): jax.ops.segment_sum(contrib, flat_ids, num_segments=tiles_column)  23 us
    all_gather x1, blocking collectives, on_device(): column = lax.all_gather(volume_own, 'orient', axis=0, tiled=True)  20 us
    gather x1, local copies, waits for them, and re-layouts, on_device(): blended_sum = jnp.sum(tile_weight[..., None] * column[tile_index], axis=0)  10.8 us
    psum x1, blocking collectives, on_device(): lax.psum(denominator.astype(jnp.bfloat16), 'frame').astype(jnp.float32)  5.15 us
  transfers between devices with their start and end apart: 2, of which 1 were waited for; matrix products, arithmetic and copies ran while one was open for 13% of the time, Pallas kernels for 0%

commit v1 on v0

v1 whole, which is shorter than its diff:
```python
import functools

import jax
import jax.numpy as jnp
from jax import lax
from jax.experimental import pallas as pl
from jax.experimental.pallas import tpu as pltpu
from jax.sharding import PartitionSpec as P

MESH = pl.DeviceIdType.MESH
F32 = jnp.float32
BF16 = jnp.bfloat16
PARTS = 4


def remote(src, dst, send_sem, recv_sem, where):
    return pltpu.make_async_remote_copy(
        src_ref=src,
        dst_ref=dst,
        send_sem=send_sem,
        recv_sem=recv_sem,
        device_id=where,
        device_id_type=MESH,
    )


def kernel(
    n_orient,
    n_frame,
    logt_hbm,
    frames_hbm,
    index_ref,
    weight_ref,
    prior_ref,
    new_log_ref,
    volume_ref,
    evidence_ref,
    logt,
    frames,
    counts,
    other,
    intensity,
    scores,
    stat_mine,
    stat_in,
    resp_out,
    resp_in,
    den_out,
    den_in,
    numer,
    spread,
    update,
    tile_out,
    tile_in,
    tiles,
    tiles_t,
    in_sem,
    count_send,
    count_recv,
    relay_send,
    relay_recv,
    resp_send,
    resp_recv,
    den_send,
    den_recv,
    fan_send,
    fan_recv,
):
    me = lax.axis_index("orient")
    mine = lax.axis_index("frame")
    rot_rows, pixels = logt.shape
    frame_rows = frames.shape[0]
    group_blocks = index_ref.shape[1]
    tile_rows, width = prior_ref.shape[1:]
    columns = pixels // n_frame
    tile_count = tile_rows * n_orient
    chunk = (384 // tile_rows if n_orient % max(384 // tile_rows, 1) == 0 else 1) * tile_rows
    core = lax.rem(me, 2)
    partner = me + 1 - 2 * core
    half = frame_rows // 2
    part = half // PARTS

    logt_copy = pltpu.make_async_copy(logt_hbm, logt, in_sem.at[0])
    logt_copy.start()
    step = frame_rows // PARTS
    frame_copies = []
    for c in range(PARTS):
        rows = pl.ds(c * step, step)
        copy = pltpu.make_async_copy(frames_hbm.at[rows], frames.at[rows], in_sem.at[1 + c])
        copy.start()
        frame_copies.append(copy)

    barrier = pltpu.get_barrier_semaphore()

    def greet(d, carry):
        pl.semaphore_signal(
            barrier, inc=1, device_id={"orient": lax.rem(me + d, n_orient)}, device_id_type=MESH
        )
        return carry

    lax.fori_loop(1, n_orient, greet, 0)
    for d in range(1, n_frame):
        pl.semaphore_signal(
            barrier, inc=1, device_id={"frame": lax.rem(mine + d, n_frame)}, device_id_type=MESH
        )

    for c in range(PARTS):
        frame_copies[c].wait()
        counts[c * step : (c + 1) * step] = (
            frames[c * step : (c + 1) * step].astype(F32).astype(BF16)
        )
    pl.semaphore_wait(barrier, n_orient - 1 + n_frame - 1)

    count_copies = []
    for d in range(1, n_frame):
        to = lax.rem(mine + d, n_frame)
        for c in range(PARTS):
            rows = pl.ds(pl.multiple_of(core * half + c * part, 16), part)
            copy = remote(
                counts.at[rows, pl.ds(pl.multiple_of(to * columns, 128), columns)],
                other.at[d - 1, rows],
                count_send.at[d - 1, c],
                count_recv.at[d - 1, c],
                {"frame": to},
            )
            copy.start()
            count_copies.append((d, c, copy))

    logt_copy.wait()
    mass = jnp.zeros((rot_rows, 128), F32)
    for c in range(pixels // 512):
        value = jnp.exp(logt[:, c * 512 : (c + 1) * 512].astype(F32))
        intensity[:, c * 512 : (c + 1) * 512] = value
        for k in range(4):
            mass = mass + value[:, k * 128 : (k + 1) * 128]
    mass = jnp.sum(mass, axis=1, keepdims=True)
    correlation = lax.dot_general(
        logt[...], counts[...], (((1,), (1,)), ((), ())), preferred_element_type=F32
    )
    score = (64.0 / pixels) * (correlation - mass)
    scores[...] = score
    peak = jnp.max(score, axis=0, keepdims=True)
    stat_mine[0:1, :] = peak
    stat_mine[1:2, :] = jnp.sum(jnp.exp(score - peak), axis=0, keepdims=True)

    def send_stat(d, carry):
        remote(
            stat_mine,
            stat_in.at[d - 1],
            fan_send.at[0],
            fan_recv.at[0],
            {"orient": lax.rem(me + d, n_orient)},
        ).start()
        return carry

    lax.fori_loop(1, n_orient, send_stat, 0)

    weight_low = weight_ref[...].astype(BF16).astype(F32)
    index = index_ref[...]
    lane = lax.broadcasted_iota(jnp.int32, (8, 128), 1)
    strip = tile_rows

    def build(o, carry):
        first = o * strip
        row_id = lax.broadcasted_iota(jnp.int32, (strip, rot_rows), 0) + first
        total = jnp.zeros((strip, rot_rows), F32)
        for j in range(group_blocks):
            value = jnp.where(row_id == index[0, j][None, :], weight_low[0, j][None, :], 0.0)
            value = value + jnp.where(
                row_id == index[1, j][None, :], weight_low[1, j][None, :], 0.0
            )
            low = value.astype(BF16)
            total = total + low.astype(F32)
            spread[o, :, j * rot_rows : (j + 1) * rot_rows] = low
        weight_sum = jnp.sum(total, axis=1, keepdims=True)
        packed = jnp.zeros((8, 128), F32)
        for b in range(tile_rows // 8):
            packed = packed + jnp.where(lane == b, weight_sum[b * 8 : (b + 1) * 8], 0.0)
        tile_out[o, tile_rows : tile_rows + 8] = packed
        return carry

    lax.fori_loop(0, n_orient, build, 0)

    fan_wait_recv = pltpu.make_async_copy(stat_in, stat_in, fan_recv.at[0])
    fan_wait_send = pltpu.make_async_copy(stat_in, stat_in, fan_send.at[0])
    fan_wait_recv.wait()
    peaks = stat_in[:, 0, :]
    totals = stat_in[:, 1, :]
    peak_mine = stat_mine[0:1, :]
    peak = jnp.maximum(jnp.max(peaks, axis=0, keepdims=True), peak_mine)
    total = stat_mine[1:2, :] * jnp.exp(peak_mine - peak) + jnp.sum(
        totals * jnp.exp(peaks - peak), axis=0, keepdims=True
    )
    evidence_ref[...] = peak + jnp.log(total)
    resp = jnp.exp(scores[...] - peak) / total
    resp_out[...] = resp.astype(BF16)
    den = jnp.sum(resp, axis=1, keepdims=True).astype(BF16)
    den_out[...] = jnp.broadcast_to(den, (rot_rows, 128))

    resp_copies = []
    for d in range(1, n_frame):
        to = {"frame": lax.rem(mine + d, n_frame)}
        copy = remote(resp_out, resp_in.at[d - 1], resp_send.at[d - 1], resp_recv.at[d - 1], to)
        copy.start()
        den_copy = remote(den_out, den_in.at[d - 1], den_send.at[d - 1], den_recv.at[d - 1], to)
        den_copy.start()
        resp_copies.append((copy, den_copy))
    fan_wait_send.wait()

    span = min(columns, 512)
    first = pl.multiple_of(mine * columns, 128)
    for c in range(columns // span):
        mixed = jnp.dot(
            resp_out[...],
            counts[:, pl.ds(pl.multiple_of(first + c * span, 128), span)],
            preferred_element_type=F32,
        )
        numer[:, c * span : (c + 1) * span] = mixed.astype(BF16).astype(F32)

    relay_copies = []
    for d, c, copy in count_copies:
        copy.wait_recv()
        rows = pl.ds(pl.multiple_of(core * half + c * part, 16), part)
        relay = remote(
            other.at[d - 1, rows],
            other.at[d - 1, rows],
            relay_send.at[d - 1, c],
            relay_recv.at[d - 1, c],
            {"orient": partner},
        )
        relay.start()
        relay_copies.append(relay)
    for copy, den_copy in resp_copies:
        copy.wait_recv()
        den_copy.wait_recv()
    for relay in relay_copies:
        relay.wait_recv()

    share = frame_rows * n_frame / (rot_rows * n_orient)
    den_all = den_out[...].astype(F32)
    for d in range(1, n_frame):
        den_all = den_all + den_in[d - 1].astype(F32)
    inverse = 1.0 / (den_all + share)
    for c in range(columns // span):
        cols = slice(c * span, (c + 1) * span)
        value = numer[:, cols]
        for d in range(1, n_frame):
            mixed = jnp.dot(resp_in[d - 1], other[d - 1, :, cols], preferred_element_type=F32)
            value = value + mixed.astype(BF16).astype(F32)
        value = value + share * intensity[:, pl.ds(pl.multiple_of(first + c * span, 128), span)]
        for k in range(span // width):
            j = c * (span // width) + k
            new = value[:, k * width : (k + 1) * width] * inverse
            high = new.astype(BF16)
            update[j * rot_rows : (j + 1) * rot_rows, 0:width] = high
            update[j * rot_rows : (j + 1) * rot_rows, width : 2 * width] = (
                new - high.astype(F32)
            ).astype(BF16)

    owners = chunk // tile_rows

    def gather_in(c, carry):
        block = spread[pl.ds(c * owners, owners)].reshape(chunk, group_blocks * rot_rows)
        summed = jnp.dot(block, update[...], preferred_element_type=F32)
        summed = summed[:, 0:width] + summed[:, width : 2 * width]
        for i in range(owners):
            tile_out[c * owners + i, 0:tile_rows] = summed[i * tile_rows : (i + 1) * tile_rows]
        return carry

    lax.fori_loop(0, tile_count // chunk, gather_in, 0)

    def send_tiles(d, carry):
        to = lax.rem(me + d, n_orient)
        remote(
            tile_out.at[to], tile_in.at[d - 1], fan_send.at[1], fan_recv.at[1], {"orient": to}
        ).start()
        return carry

    lax.fori_loop(1, n_orient, send_tiles, 0)
    pltpu.make_async_copy(tile_in, tile_in, fan_recv.at[1]).wait()
    whole = lax.fori_loop(0, n_orient - 1, lambda d, so_far: so_far + tile_in[d], tile_out[me])
    prior_weight = rot_rows * group_blocks / (4.0 * tile_rows)
    base = pl.multiple_of(me * tile_rows, 8)
    for b in range(tile_rows // 8):
        weight = whole[tile_rows : tile_rows + 8, b : b + 1]
        rows = slice(b * 8, (b + 1) * 8)
        value = (whole[rows] + prior_weight * prior_ref[0, rows]) / (weight + prior_weight)
        volume_ref[0, rows] = value
        tiles[pl.ds(base + b * 8, 8)] = value

    def send_volume(d, carry):
        own = tiles.at[pl.ds(base, tile_rows)]
        remote(
            own, own, fan_send.at[2], fan_recv.at[2], {"orient": lax.rem(me + d, n_orient)}
        ).start()
        return carry

    lax.fori_loop(1, n_orient, send_volume, 0)
    for d, c, copy in count_copies:
        copy.wait_send()
    for relay in relay_copies:
        relay.wait_send()
    for copy, den_copy in resp_copies:
        copy.wait_send()
        den_copy.wait_send()
    pltpu.make_async_copy(tile_in, tile_in, fan_send.at[1]).wait()
    incoming = tiles.at[pl.ds(0, tile_count - tile_rows)]
    pltpu.make_async_copy(incoming, incoming, fan_recv.at[2]).wait()

    def turn(c, carry):
        at = pl.multiple_of(c * 128, 128)
        value = tiles[pl.ds(at, 128)].T
        high = value.astype(BF16)
        tiles_t[0:width, pl.ds(at, 128)] = high
        tiles_t[width : 2 * width, pl.ds(at, 128)] = (value - high.astype(F32)).astype(BF16)
        return carry

    lax.fori_loop(0, tile_count // 128, turn, 0)
    both = weight_low[0] + weight_low[1]
    both = jnp.where(index[0] == index[1], both.astype(BF16).astype(F32), both)
    scale = 1.0 / both
    pair = 2 if group_blocks % 2 == 0 else 1
    for c in range(group_blocks // pair):
        cols = slice(c * pair * rot_rows, (c + 1) * pair * rot_rows)
        block = spread[:, :, cols].reshape(tile_count, pair * rot_rows)
        blended = jnp.dot(tiles_t[...], block, preferred_element_type=F32)
        blended = blended[0:width] + blended[width : 2 * width]
        for k in range(pair):
            j = c * pair + k
            value = jnp.log(blended[:, k * rot_rows : (k + 1) * rot_rows] * scale[j][None, :])
            new_log_ref[:, j * width : (j + 1) * width] = value.T.astype(BF16)
    pltpu.make_async_copy(incoming, incoming, fan_send.at[2]).wait()


def on_device(log_tomograms, frames, tile_index, tile_weight, prior_volume):
    n_orient = lax.axis_size("orient")
    n_frame = lax.axis_size("frame")
    rot_rows, pixels = log_tomograms.shape
    frame_rows = frames.shape[0]
    group_blocks = tile_index.shape[1]
    tile_rows, width = prior_volume.shape[1:]
    columns = pixels // n_frame
    tile_count = tile_rows * n_orient
    others = max(n_frame - 1, 1)
    dma = pltpu.SemaphoreType.DMA
    vmem = pl.BlockSpec(memory_space=pltpu.VMEM)
    anywhere = pl.BlockSpec(memory_space=pl.ANY)
    new_log, volume, evidence = pl.pallas_call(
        functools.partial(kernel, n_orient, n_frame),
        out_shape=(
            jax.ShapeDtypeStruct((rot_rows, columns), BF16),
            jax.ShapeDtypeStruct((1, tile_rows, width), F32),
            jax.ShapeDtypeStruct((1, frame_rows), F32),
        ),
        in_specs=[anywhere, anywhere, vmem, vmem, vmem],
        out_specs=(vmem, vmem, vmem),
        scratch_shapes=[
            pltpu.VMEM((rot_rows, pixels), BF16),
            pltpu.VMEM((frame_rows, pixels), jnp.int32),
            pltpu.VMEM((frame_rows, pixels), BF16),
            pltpu.VMEM((others, frame_rows, columns), BF16),
            pltpu.VMEM((rot_rows, pixels), F32),
            pltpu.VMEM((rot_rows, frame_rows), F32),
            pltpu.VMEM((2, frame_rows), F32),
            pltpu.VMEM((n_orient - 1, 2, frame_rows), F32),
            pltpu.VMEM((rot_rows, frame_rows), BF16),
            pltpu.VMEM((others, rot_rows, frame_rows), BF16),
            pltpu.VMEM((rot_rows, 128), BF16),
            pltpu.VMEM((others, rot_rows, 128), BF16),
            pltpu.VMEM((rot_rows, columns), F32),
            pltpu.VMEM((n_orient, tile_rows, group_blocks * rot_rows), BF16),
            pltpu.VMEM((group_blocks * rot_rows, 2 * width), BF16),
            pltpu.VMEM((n_orient, tile_rows + 8, width), F32),
            pltpu.VMEM((n_orient - 1, tile_rows + 8, width), F32),
            pltpu.VMEM((tile_count, width), F32),
            pltpu.VMEM((2 * width, tile_count), BF16),
            dma((1 + PARTS,)),
            dma((others, PARTS)),
            dma((others, PARTS)),
            dma((others, PARTS)),
            dma((others, PARTS)),
            dma((others,)),
            dma((others,)),
            dma((others,)),
            dma((others,)),
            dma((3,)),
            dma((3,)),
        ],
        compiler_params=pltpu.CompilerParams(
            collective_id=0, has_side_effects=True, vmem_limit_bytes=60 * 1024 * 1024
        ),
    )(log_tomograms, frames, tile_index, tile_weight, prior_volume)
    return (new_log, volume, evidence.reshape(frame_rows))


def solution(mesh):
    placed = (
        P("orient", None),
        P("frame", None),
        P(None, "frame", "orient"),
        P(None, "frame", "orient"),
        P("frame", "orient", None),
    )
    return jax.shard_map(
        on_device,
        mesh=mesh,
        in_specs=placed,
        out_specs=(P("orient", "frame"), P("frame", "orient", None), P("frame")),
        check_vma=False,
    )
```

time: 241 us -> 43.7 us (0.18)
  blocking collectives: 96.1 us -> 0 us
  other arithmetic: 58.3 us -> 0 us
  waiting for transfers between devices: 50.6 us -> 0 us
  Pallas kernels: 0 us -> 38.3 us
  between operations: 14.9 us -> 0.64 us
  local copies, waits for them, and re-layouts: 13.4 us -> 4.42 us
  matrix products: 6.79 us -> 0 us
    all_gather x3 -> x0, blocking collectives: 60.6 us -> none  [the longest x2 40.6 us: merged(): pieces = jax.tree.map(lambda part: lax.all_gather(part, axis), value)]
    scatter-add x2 -> x0, other arithmetic: 51.8 us -> none  [the longest x1 28.8 us: on_device(): jax.ops.segment_sum(tile_weight.reshape(-1), flat_ids, num_segments=tiles...]
    unnamed x3 -> x0, waiting for transfers between devices: 50.6 us -> none
    pallas_call x0 -> x1, Pallas kernels: none -> 38.3 us  [on_device(): pl.pallas_call(functools.partial(kernel, n_orient, n_frame), out_shape=(j...]
    unnamed x1 -> x0, blocking collectives: 30.3 us -> none
    gather x1 -> x0, local copies, waits for them, and re-layouts: 10.8 us -> none  [on_device(): blended_sum = jnp.sum(tile_weight[..., None] * column[tile_index], axis=0)]
    dot_general x2 -> x0, matrix products: 6.79 us -> none  [the longest x1 3.72 us: on_device(): numerator = jnp.dot(resp_low, counts, preferred_element_type=jnp.float32)]
    psum x1 -> x0, blocking collectives: 5.15 us -> none  [on_device(): lax.psum(denominator.astype(jnp.bfloat16), 'frame').astype(jnp.float32)]
  transfers between devices with their start and end apart: 2 -> 0, of which waited for: 1 -> 0; matrix products, arithmetic and copies ran while one was open for 13% -> 0% of each run, Pallas kernels for 0% -> 0%
where the time goes in v1:
time: 43.7 us; the launch traced here: 43.3 us
  Pallas kernels  38.3 us (88%)
  local copies, waits for them, and re-layouts  4.42 us (10%)
  between operations  0.64 us (1%)
    pallas_call x1, Pallas kernels, on_device(): pl.pallas_call(functools.partial(kernel, n_orient, n_frame), out_shape=(j...  38.3 us
    unnamed x3, local copies, waits for them, and re-layouts  4.42 us

profile of v1, /device:TPU:0, one launch (start us, length us, event | category | flops | bytes accessed | tf_op | source)
XLA Modules:
  0.0 43.3 jit_solution(194112451879409812)
XLA Ops:
  0.6 38.3 %shard_map.76 = (bf16[128,2048]{1,0:T(8,128)(2,1)}, f32[1,24,128]{2,1,0:T(8,128)}, f32[1,256]{1,0:T(1,128)}) custom-call(bf16[128,4096]{1,0:T(8,128)(2,1)} %logt_hbm.1, s32[256,4096]{1,0:T(8,128)} %frames_hbm.1, s32[2,16,128]{2,1,0:T(8,128)} %index_ref.1, f32[2,16,128]{2,1,0:T(8,128)} %weight_ref.1, f32[1,24,128]{2,1,0:T(8,128)} %prior_ref.1), custom_call_target="tpu_custom_call" | custom-call | tf_op jit(solution)/shard_map/pallas_call | solution.py:348
  38.9 1.9 %copy.11 = bf16[128,2048]{1,0:T(8,128)(2,1)} copy(bf16[128,2048]{1,0:T(8,128)(2,1)} %get-tuple-element.12) | data formatting | bytes 1048576
  40.8 1.3 %copy.12 = f32[1,24,128]{2,1,0:T(8,128)} copy(f32[1,24,128]{2,1,0:T(8,128)} %get-tuple-element.13) | data formatting | bytes 24576
  42.1 1.2 %copy.13 = f32[256]{0:T(256)} copy(f32[256]{0:T(256)} %bitcast.1) | data formatting | bytes 2048

commit v2 on v1

--- a/solution.py
+++ b/solution.py
@@ -29,14 +29,17 @@
     n_frame,
     logt_hbm,
     frames_hbm,
-    index_ref,
-    weight_ref,
-    prior_ref,
+    index_hbm,
+    weight_hbm,
+    prior_hbm,
     new_log_ref,
     volume_ref,
     evidence_ref,
     logt,
     frames,
+    index_ref,
+    weight_ref,
+    prior_ref,
     counts,
     other,
     intensity,
@@ -75,10 +78,10 @@
     columns = pixels // n_frame
     tile_count = tile_rows * n_orient
     chunk = (384 // tile_rows if n_orient % max(384 // tile_rows, 1) == 0 else 1) * tile_rows
-    core = lax.rem(me, 2)
-    partner = me + 1 - 2 * core
-    half = frame_rows // 2
-    part = half // PARTS
+    partner = me + 1 - 2 * lax.rem(me, 2)
+    across = me + 2 - 4 * lax.rem(me // 2, 2)
+    fourth = frame_rows // 4
+    part = fourth // PARTS
 
     logt_copy = pltpu.make_async_copy(logt_hbm, logt, in_sem.at[0])
     logt_copy.start()
@@ -90,6 +93,14 @@
         copy.start()
         frame_copies.append(copy)
 
+    small_copies = []
+    for i, (source, target) in enumerate(
+        ((index_hbm, index_ref), (weight_hbm, weight_ref), (prior_hbm, prior_ref))
+    ):
+        copy = pltpu.make_async_copy(source, target, in_sem.at[1 + PARTS + i])
+        copy.start()
+        small_copies.append(copy)
+
     barrier = pltpu.get_barrier_semaphore()
 
     def greet(d, carry):
@@ -109,23 +120,6 @@
         counts[c * step : (c + 1) * step] = (
             frames[c * step : (c + 1) * step].astype(F32).astype(BF16)
         )
-    pl.semaphore_wait(barrier, n_orient - 1 + n_frame - 1)
-
-    count_copies = []
-    for d in range(1, n_frame):
-        to = lax.rem(mine + d, n_frame)
-        for c in range(PARTS):
-            rows = pl.ds(pl.multiple_of(core * half + c * part, 16), part)
-            copy = remote(
-                counts.at[rows, pl.ds(pl.multiple_of(to * columns, 128), columns)],
-                other.at[d - 1, rows],
-                count_send.at[d - 1, c],
-                count_recv.at[d - 1, c],
-                {"frame": to},
-            )
-            copy.start()
-            count_copies.append((d, c, copy))
-
     logt_copy.wait()
     mass = jnp.zeros((rot_rows, 128), F32)
     for c in range(pixels // 512):
@@ -143,6 +137,25 @@
     stat_mine[0:1, :] = peak
     stat_mine[1:2, :] = jnp.sum(jnp.exp(score - peak), axis=0, keepdims=True)
 
+    pl.semaphore_wait(barrier, n_orient - 1 + n_frame - 1)
+
+    def quarter(owner, c):
+        return pl.ds(pl.multiple_of(lax.rem(owner, 4) * fourth + c * part, 16), part)
+
+    count_copies = []
+    for c in range(PARTS):
+        for d in range(1, n_frame):
+            to = lax.rem(mine + d, n_frame)
+            copy = remote(
+                counts.at[quarter(me, c), pl.ds(pl.multiple_of(to * columns, 128), columns)],
+                other.at[d - 1, quarter(me, c)],
+                count_send.at[d - 1, c],
+                count_recv.at[d - 1, c],
+                {"frame": to},
+            )
+            copy.start()
+            count_copies.append((d, c, copy))
+
     def send_stat(d, carry):
         remote(
             stat_mine,
@@ -155,10 +168,14 @@
 
     lax.fori_loop(1, n_orient, send_stat, 0)
 
+    for copy in small_copies:
+        copy.wait()
+
     weight_low = weight_ref[...].astype(BF16).astype(F32)
     index = index_ref[...]
     lane = lax.broadcasted_iota(jnp.int32, (8, 128), 1)
-    strip = tile_rows
+    joint = spread.shape[1] // tile_rows
+    strip = joint * tile_rows
 
     def build(o, carry):
         first = o * strip
@@ -173,13 +190,44 @@
             total = total + low.astype(F32)
             spread[o, :, j * rot_rows : (j + 1) * rot_rows] = low
         weight_sum = jnp.sum(total, axis=1, keepdims=True)
-        packed = jnp.zeros((8, 128), F32)
-        for b in range(tile_rows // 8):
-            packed = packed + jnp.where(lane == b, weight_sum[b * 8 : (b + 1) * 8], 0.0)
-        tile_out[o, tile_rows : tile_rows + 8] = packed
-        return carry
-
-    lax.fori_loop(0, n_orient, build, 0)
+        for i in range(joint):
+            packed = jnp.zeros((8, 128), F32)
+            for b in range(tile_rows // 8):
+                at = i * tile_rows + b * 8
+                packed = packed + jnp.where(lane == b, weight_sum[at : at + 8], 0.0)
+            tile_out[o * joint + i, tile_rows : tile_rows + 8] = packed
+        return carry
+
+    lax.fori_loop(0, n_orient // joint, build, 0)
+
+    relay_copies = []
+
+    def relay(owner, d, c, kind, to):
+        where = other.at[d - 1, quarter(owner, c)]
+        copy = remote(
+            where,
+            where,
+            relay_send.at[kind, d - 1, c],
+            relay_recv.at[kind, d - 1, c],
+            {"orient": to},
+        )
+        copy.start()
+        relay_copies.append((kind, d, c, copy))
+
+    def relay_first(start, stop):
+        for d, c, copy in count_copies:
+            if start <= c < stop:
+                copy.wait_recv()
+                relay(me, d, c, 0, across)
+                relay(me, d, c, 1, partner)
+
+    def relay_second(start, stop):
+        for kind, d, c, copy in list(relay_copies):
+            if kind == 0 and start <= c < stop:
+                copy.wait_recv()
+                relay(across, d, c, 2, partner)
+
+    relay_first(0, 2)
 
     fan_wait_recv = pltpu.make_async_copy(stat_in, stat_in, fan_recv.at[0])
     fan_wait_send = pltpu.make_async_copy(stat_in, stat_in, fan_send.at[0])
@@ -217,24 +265,14 @@
         )
         numer[:, c * span : (c + 1) * span] = mixed.astype(BF16).astype(F32)
 
-    relay_copies = []
-    for d, c, copy in count_copies:
-        copy.wait_recv()
-        rows = pl.ds(pl.multiple_of(core * half + c * part, 16), part)
-        relay = remote(
-            other.at[d - 1, rows],
-            other.at[d - 1, rows],
-            relay_send.at[d - 1, c],
-            relay_recv.at[d - 1, c],
-            {"orient": partner},
-        )
-        relay.start()
-        relay_copies.append(relay)
+    relay_first(2, PARTS)
+    relay_second(0, PARTS)
     for copy, den_copy in resp_copies:
         copy.wait_recv()
         den_copy.wait_recv()
-    for relay in relay_copies:
-        relay.wait_recv()
+    for kind, d, c, copy in relay_copies:
+        if kind > 0:
+            copy.wait_recv()
 
     share = frame_rows * n_frame / (rot_rows * n_orient)
     den_all = den_out[...].astype(F32)
@@ -260,7 +298,7 @@
     owners = chunk // tile_rows
 
     def gather_in(c, carry):
-        block = spread[pl.ds(c * owners, owners)].reshape(chunk, group_blocks * rot_rows)
+        block = spread[pl.ds(c * (chunk // strip), chunk // strip)].reshape(chunk, group_blocks * rot_rows)
         summed = jnp.dot(block, update[...], preferred_element_type=F32)
         summed = summed[:, 0:width] + summed[:, width : 2 * width]
         for i in range(owners):
@@ -298,8 +336,8 @@
     lax.fori_loop(1, n_orient, send_volume, 0)
     for d, c, copy in count_copies:
         copy.wait_send()
-    for relay in relay_copies:
-        relay.wait_send()
+    for kind, d, c, copy in relay_copies:
+        copy.wait_send()
     for copy, den_copy in resp_copies:
         copy.wait_send()
         den_copy.wait_send()
@@ -332,6 +370,17 @@
     pltpu.make_async_copy(incoming, incoming, fan_send.at[2]).wait()
 
 
+def place(a_in, b_in, c_in, a_out, b_out, c_out, sem):
+    copies = [
+        pltpu.make_async_copy(source, target, sem.at[i])
+        for i, (source, target) in enumerate(((a_in, a_out), (b_in, b_out), (c_in, c_out)))
+    ]
+    for copy in copies:
+        copy.start()
+    for copy in copies:
+        copy.wait()
+
+
 def on_device(log_tomograms, frames, tile_index, tile_weight, prior_volume):
     n_orient = lax.axis_size("orient")
     n_frame = lax.axis_size("frame")
@@ -344,19 +393,22 @@
     others = max(n_frame - 1, 1)
     dma = pltpu.SemaphoreType.DMA
     vmem = pl.BlockSpec(memory_space=pltpu.VMEM)
-    anywhere = pl.BlockSpec(memory_space=pl.ANY)
+    hbm = pl.BlockSpec(memory_space=pltpu.HBM)
     new_log, volume, evidence = pl.pallas_call(
         functools.partial(kernel, n_orient, n_frame),
         out_shape=(
-            jax.ShapeDtypeStruct((rot_rows, columns), BF16),
-            jax.ShapeDtypeStruct((1, tile_rows, width), F32),
-            jax.ShapeDtypeStruct((1, frame_rows), F32),
+            pltpu.VMEM((rot_rows, columns), BF16),
+            pltpu.VMEM((1, tile_rows, width), F32),
+            pltpu.VMEM((1, frame_rows), F32),
         ),
-        in_specs=[anywhere, anywhere, vmem, vmem, vmem],
+        in_specs=[hbm] * 5,
         out_specs=(vmem, vmem, vmem),
         scratch_shapes=[
             pltpu.VMEM((rot_rows, pixels), BF16),
             pltpu.VMEM((frame_rows, pixels), jnp.int32),
+            pltpu.VMEM(tile_index.shape, jnp.int32),
+            pltpu.VMEM(tile_weight.shape, F32),
+            pltpu.VMEM(prior_volume.shape, F32),
             pltpu.VMEM((frame_rows, pixels), BF16),
             pltpu.VMEM((others, frame_rows, columns), BF16),
             pltpu.VMEM((rot_rows, pixels), F32),
@@ -368,17 +420,17 @@
             pltpu.VMEM((rot_rows, 128), BF16),
             pltpu.VMEM((others, rot_rows, 128), BF16),
             pltpu.VMEM((rot_rows, columns), F32),
-            pltpu.VMEM((n_orient, tile_rows, group_blocks * rot_rows), BF16),
+            pltpu.VMEM((n_orient // 2, 2 * tile_rows, group_blocks * rot_rows), BF16),
             pltpu.VMEM((group_blocks * rot_rows, 2 * width), BF16),
             pltpu.VMEM((n_orient, tile_rows + 8, width), F32),
             pltpu.VMEM((n_orient - 1, tile_rows + 8, width), F32),
             pltpu.VMEM((tile_count, width), F32),
             pltpu.VMEM((2 * width, tile_count), BF16),
-            dma((1 + PARTS,)),
+            dma((4 + PARTS,)),
             dma((others, PARTS)),
             dma((others, PARTS)),
-            dma((others, PARTS)),
-            dma((others, PARTS)),
+            dma((3, others, PARTS)),
+            dma((3, others, PARTS)),
             dma((others,)),
             dma((others,)),
             dma((others,)),
@@ -387,9 +439,21 @@
             dma((3,)),
         ],
         compiler_params=pltpu.CompilerParams(
-            collective_id=0, has_side_effects=True, vmem_limit_bytes=60 * 1024 * 1024
+            collective_id=0, has_side_effects=True, vmem_limit_bytes=48 * 1024 * 1024
         ),
-    )(log_tomograms, frames, tile_index, tile_weight, prior_volume)
+    )(*(
+        pltpu.with_memory_space_constraint(value, pltpu.HBM)
+        for value in (log_tomograms, frames, tile_index, tile_weight, prior_volume)
+    ))
+    made = (new_log, volume, evidence)
+    new_log, volume, evidence = pl.pallas_call(
+        place,
+        out_shape=tuple(jax.ShapeDtypeStruct(value.shape, value.dtype) for value in made),
+        in_specs=[vmem] * 3,
+        out_specs=(hbm,) * 3,
+        scratch_shapes=[dma((3,))],
+        compiler_params=pltpu.CompilerParams(vmem_limit_bytes=4 * 1024 * 1024),
+    )(*made)
     return (new_log, volume, evidence.reshape(frame_rows))
 
 

time: 43.7 us -> 36.6 us (0.84)
  local copies, waits for them, and re-layouts: 4.42 us -> 0 us
  Pallas kernels: 38.3 us -> 35.8 us
    unnamed x3 -> x0, local copies, waits for them, and re-layouts: 4.42 us -> none
    pallas_call x1 -> x2, Pallas kernels: 38.3 us -> 35.8 us  [the longest x1 35 us: on_device(): pl.pallas_call(functools.partial(kernel, n_orient, n_frame), out_shape=(p...]
where the time goes in v2:
time: 36.6 us; the launch traced here: 36.4 us
  Pallas kernels  35.8 us (98%)
  between operations  0.64 us (2%)
    pallas_call x1, Pallas kernels, on_device(): pl.pallas_call(functools.partial(kernel, n_orient, n_frame), out_shape=(p...  35 us
    pallas_call x1, Pallas kernels, on_device(): pl.pallas_call(place, out_shape=tuple((jax.ShapeDtypeStruct(value.shape,...  0.83 us

profile of v2, /device:TPU:0, one launch (start us, length us, event | category | flops | bytes accessed | tf_op | source)
XLA Modules:
  0.0 36.4 jit_solution(16417580432947274322)
XLA Ops:
  0.6 35.0 %shard_map.76 = (bf16[128,2048]{1,0:T(8,128)(2,1)S(1)}, f32[1,24,128]{2,1,0:T(8,128)S(1)}, f32[1,256]{1,0:T(1,128)S(1)}) custom-call(bf16[128,4096]{1,0:T(8,128)(2,1)} %logt_hbm.1, s32[256,4096]{1,0:T(8,128)} %frames_hbm.1, s32[2,16,128]{2,1,0:T(8,128)} %index_hbm.1, f32[2,16,128]{2,1,0:T(8,128)} %weight_hbm.1, f32[1,24,128]{2,1,0:T(8,128)} %prior_hbm.1), custom_call_target="tpu_custom_call" | custom-call | tf_op jit(solution)/shard_map/pallas_call | solution.py:397
  35.6 0.8 %shard_map.77 = (bf16[128,2048]{1,0:T(8,128)(2,1)}, f32[1,24,128]{2,1,0:T(8,128)}, f32[1,256]{1,0:T(1,128)}) custom-call(bf16[128,2048]{1,0:T(8,128)(2,1)S(1)} %get-tuple-element.9.a_in, f32[1,24,128]{2,1,0:T(8,128)S(1)} %get-tuple-element.10.b_in, f32[1,256]{1,0:T(1,128)S(1)} %get-tuple-element.11.c_in), custom_call_target="tpu_custom_call" | custom-call | tf_op jit(solution)/shard_map/pallas_call | solution.py:449

commit v3 on v2

--- a/solution.py
+++ b/solution.py
@@ -53,6 +53,7 @@
     numer,
     spread,
     update,
+    sums,
     tile_out,
     tile_in,
     tiles,
@@ -194,8 +195,11 @@
             packed = jnp.zeros((8, 128), F32)
             for b in range(tile_rows // 8):
                 at = i * tile_rows + b * 8
-                packed = packed + jnp.where(lane == b, weight_sum[at : at + 8], 0.0)
-            tile_out[o * joint + i, tile_rows : tile_rows + 8] = packed
+                exact = weight_sum[at : at + 8]
+                high = exact.astype(BF16).astype(F32)
+                packed = packed + jnp.where(lane == b, high, 0.0)
+                packed = packed + jnp.where(lane == 64 + b, exact - high, 0.0)
+            sums[o * joint + i] = packed
         return carry
 
     lax.fori_loop(0, n_orient // joint, build, 0)
@@ -302,7 +306,9 @@
         summed = jnp.dot(block, update[...], preferred_element_type=F32)
         summed = summed[:, 0:width] + summed[:, width : 2 * width]
         for i in range(owners):
-            tile_out[c * owners + i, 0:tile_rows] = summed[i * tile_rows : (i + 1) * tile_rows]
+            own = summed[i * tile_rows : (i + 1) * tile_rows]
+            message = jnp.concatenate([own, sums[c * owners + i]], axis=0)
+            tile_out[c * owners + i] = message.astype(BF16)
         return carry
 
     lax.fori_loop(0, tile_count // chunk, gather_in, 0)
@@ -316,18 +322,20 @@
 
     lax.fori_loop(1, n_orient, send_tiles, 0)
     pltpu.make_async_copy(tile_in, tile_in, fan_recv.at[1]).wait()
-    whole = lax.fori_loop(0, n_orient - 1, lambda d, so_far: so_far + tile_in[d], tile_out[me])
+    whole = lax.fori_loop(0, n_orient - 1, lambda d, so_far: so_far + tile_in[d].astype(F32), tile_out[me].astype(F32))
     prior_weight = rot_rows * group_blocks / (4.0 * tile_rows)
-    base = pl.multiple_of(me * tile_rows, 8)
-    for b in range(tile_rows // 8):
-        weight = whole[tile_rows : tile_rows + 8, b : b + 1]
-        rows = slice(b * 8, (b + 1) * 8)
-        value = (whole[rows] + prior_weight * prior_ref[0, rows]) / (weight + prior_weight)
-        volume_ref[0, rows] = value
-        tiles[pl.ds(base + b * 8, 8)] = value
+    weight = [
+        whole[tile_rows:, b : b + 1] + whole[tile_rows:, 64 + b : 65 + b]
+        for b in range(tile_rows // 8)
+    ]
+    weight = jnp.concatenate(weight, axis=0)
+    value = whole[0:tile_rows] + prior_weight * prior_ref[0]
+    value = value / (weight + prior_weight)
+    volume_ref[0] = value
+    tiles[me] = (value - 1.0).astype(BF16)
 
     def send_volume(d, carry):
-        own = tiles.at[pl.ds(base, tile_rows)]
+        own = tiles.at[me]
         remote(
             own, own, fan_send.at[2], fan_recv.at[2], {"orient": lax.rem(me + d, n_orient)}
         ).start()
@@ -342,18 +350,15 @@
         copy.wait_send()
         den_copy.wait_send()
     pltpu.make_async_copy(tile_in, tile_in, fan_send.at[1]).wait()
-    incoming = tiles.at[pl.ds(0, tile_count - tile_rows)]
+    incoming = tiles.at[pl.ds(0, n_orient - 1)]
     pltpu.make_async_copy(incoming, incoming, fan_recv.at[2]).wait()
 
     def turn(c, carry):
-        at = pl.multiple_of(c * 128, 128)
-        value = tiles[pl.ds(at, 128)].T
-        high = value.astype(BF16)
-        tiles_t[0:width, pl.ds(at, 128)] = high
-        tiles_t[width : 2 * width, pl.ds(at, 128)] = (value - high.astype(F32)).astype(BF16)
-        return carry
-
-    lax.fori_loop(0, tile_count // 128, turn, 0)
+        value = tiles[pl.ds(c * owners, owners)].astype(F32).reshape(chunk, width)
+        tiles_t[:, pl.ds(pl.multiple_of(c * chunk, 128), chunk)] = value.T.astype(BF16)
+        return carry
+
+    lax.fori_loop(0, tile_count // chunk, turn, 0)
     both = weight_low[0] + weight_low[1]
     both = jnp.where(index[0] == index[1], both.astype(BF16).astype(F32), both)
     scale = 1.0 / both
@@ -362,10 +367,10 @@
         cols = slice(c * pair * rot_rows, (c + 1) * pair * rot_rows)
         block = spread[:, :, cols].reshape(tile_count, pair * rot_rows)
         blended = jnp.dot(tiles_t[...], block, preferred_element_type=F32)
-        blended = blended[0:width] + blended[width : 2 * width]
         for k in range(pair):
             j = c * pair + k
-            value = jnp.log(blended[:, k * rot_rows : (k + 1) * rot_rows] * scale[j][None, :])
+            value = blended[:, k * rot_rows : (k + 1) * rot_rows] * scale[j][None, :]
+            value = jnp.log(1.0 + value)
             new_log_ref[:, j * width : (j + 1) * width] = value.T.astype(BF16)
     pltpu.make_async_copy(incoming, incoming, fan_send.at[2]).wait()
 
@@ -422,10 +427,11 @@
             pltpu.VMEM((rot_rows, columns), F32),
             pltpu.VMEM((n_orient // 2, 2 * tile_rows, group_blocks * rot_rows), BF16),
             pltpu.VMEM((group_blocks * rot_rows, 2 * width), BF16),
-            pltpu.VMEM((n_orient, tile_rows + 8, width), F32),
-            pltpu.VMEM((n_orient - 1, tile_rows + 8, width), F32),
-            pltpu.VMEM((tile_count, width), F32),
-            pltpu.VMEM((2 * width, tile_count), BF16),
+            pltpu.VMEM((n_orient, 8, width), F32),
+            pltpu.VMEM((n_orient, tile_rows + 8, width), BF16),
+            pltpu.VMEM((n_orient - 1, tile_rows + 8, width), BF16),
+            pltpu.VMEM((n_orient, tile_rows, width), BF16),
+            pltpu.VMEM((width, tile_count), BF16),
             dma((4 + PARTS,)),
             dma((others, PARTS)),
             dma((others, PARTS)),

time: 36.6 us -> 33.2 us (0.907)
  Pallas kernels: 35.8 us -> 32.4 us
    pallas_call x1, Pallas kernels: 35 us -> 31.5 us  [on_device(): pl.pallas_call(functools.partial(kernel, n_orient, n_frame), out_shape=(p...]
where the time goes in v3:
time: 33.2 us; the launch traced here: 33 us
  Pallas kernels  32.4 us (98%)
  between operations  0.64 us (2%)
    pallas_call x1, Pallas kernels, on_device(): pl.pallas_call(functools.partial(kernel, n_orient, n_frame), out_shape=(p...  31.5 us
    pallas_call x1, Pallas kernels, on_device(): pl.pallas_call(place, out_shape=tuple((jax.ShapeDtypeStruct(value.shape,...  0.83 us

profile of v3, /device:TPU:0, one launch (start us, length us, event | category | flops | bytes accessed | tf_op | source)
XLA Modules:
  0.0 33.0 jit_solution(11205624788964185018)
XLA Ops:
  0.6 31.5 %shard_map.76 = (bf16[128,2048]{1,0:T(8,128)(2,1)S(1)}, f32[1,24,128]{2,1,0:T(8,128)S(1)}, f32[1,256]{1,0:T(1,128)S(1)}) custom-call(bf16[128,4096]{1,0:T(8,128)(2,1)} %logt_hbm.1, s32[256,4096]{1,0:T(8,128)} %frames_hbm.1, s32[2,16,128]{2,1,0:T(8,128)} %index_hbm.1, f32[2,16,128]{2,1,0:T(8,128)} %weight_hbm.1, f32[1,24,128]{2,1,0:T(8,128)} %prior_hbm.1), custom_call_target="tpu_custom_call" | custom-call | tf_op jit(solution)/shard_map/pallas_call | solution.py:402
  32.2 0.8 %shard_map.77 = (bf16[128,2048]{1,0:T(8,128)(2,1)}, f32[1,24,128]{2,1,0:T(8,128)}, f32[1,256]{1,0:T(1,128)}) custom-call(bf16[128,2048]{1,0:T(8,128)(2,1)S(1)} %get-tuple-element.9.a_in, f32[1,24,128]{2,1,0:T(8,128)S(1)} %get-tuple-element.10.b_in, f32[1,256]{1,0:T(1,128)S(1)} %get-tuple-element.11.c_in), custom_call_target="tpu_custom_call" | custom-call | tf_op jit(solution)/shard_map/pallas_call | solution.py:455

commit v4 on v3

--- a/solution.py
+++ b/solution.py
@@ -82,6 +82,14 @@
     partner = me + 1 - 2 * lax.rem(me, 2)
     across = me + 2 - 4 * lax.rem(me // 2, 2)
     fourth = frame_rows // 4
+
+    def fan_out(send):
+        if n_orient <= 32:
+            for d in sorted(range(1, n_orient), key=lambda d: abs(2 * d - n_orient)):
+                send(d, 0)
+        else:
+            lax.fori_loop(1, n_orient, send, 0)
+
     part = fourth // PARTS
 
     logt_copy = pltpu.make_async_copy(logt_hbm, logt, in_sem.at[0])
@@ -110,7 +118,7 @@
         )
         return carry
 
-    lax.fori_loop(1, n_orient, greet, 0)
+    fan_out(greet)
     for d in range(1, n_frame):
         pl.semaphore_signal(
             barrier, inc=1, device_id={"frame": lax.rem(mine + d, n_frame)}, device_id_type=MESH
@@ -140,6 +148,18 @@
 
     pl.semaphore_wait(barrier, n_orient - 1 + n_frame - 1)
 
+    def send_stat(d, carry):
+        remote(
+            stat_mine,
+            stat_in.at[d - 1],
+            fan_send.at[0],
+            fan_recv.at[0],
+            {"orient": lax.rem(me + d, n_orient)},
+        ).start()
+        return carry
+
+    fan_out(send_stat)
+
     def quarter(owner, c):
         return pl.ds(pl.multiple_of(lax.rem(owner, 4) * fourth + c * part, 16), part)
 
@@ -156,18 +176,6 @@
             )
             copy.start()
             count_copies.append((d, c, copy))
-
-    def send_stat(d, carry):
-        remote(
-            stat_mine,
-            stat_in.at[d - 1],
-            fan_send.at[0],
-            fan_recv.at[0],
-            {"orient": lax.rem(me + d, n_orient)},
-        ).start()
-        return carry
-
-    lax.fori_loop(1, n_orient, send_stat, 0)
 
     for copy in small_copies:
         copy.wait()
@@ -261,16 +269,23 @@
 
     span = min(columns, 512)
     first = pl.multiple_of(mine * columns, 128)
-    for c in range(columns // span):
-        mixed = jnp.dot(
-            resp_out[...],
-            counts[:, pl.ds(pl.multiple_of(first + c * span, 128), span)],
-            preferred_element_type=F32,
-        )
-        numer[:, c * span : (c + 1) * span] = mixed.astype(BF16).astype(F32)
-
-    relay_first(2, PARTS)
-    relay_second(0, PARTS)
+    pieces = columns // span
+
+    def own_sums(start, stop):
+        for c in range(start, stop):
+            mixed = jnp.dot(
+                resp_out[...],
+                counts[:, pl.ds(pl.multiple_of(first + c * span, 128), span)],
+                preferred_element_type=F32,
+            )
+            numer[:, c * span : (c + 1) * span] = mixed.astype(BF16).astype(F32)
+
+    relay_first(2, 3)
+    own_sums(0, pieces // 2)
+    relay_first(3, PARTS)
+    relay_second(0, 2)
+    own_sums(pieces // 2, pieces)
+    relay_second(2, PARTS)
     for copy, den_copy in resp_copies:
         copy.wait_recv()
         den_copy.wait_recv()
@@ -320,7 +335,7 @@
         ).start()
         return carry
 
-    lax.fori_loop(1, n_orient, send_tiles, 0)
+    fan_out(send_tiles)
     pltpu.make_async_copy(tile_in, tile_in, fan_recv.at[1]).wait()
     whole = lax.fori_loop(0, n_orient - 1, lambda d, so_far: so_far + tile_in[d].astype(F32), tile_out[me].astype(F32))
     prior_weight = rot_rows * group_blocks / (4.0 * tile_rows)
@@ -341,7 +356,7 @@
         ).start()
         return carry
 
-    lax.fori_loop(1, n_orient, send_volume, 0)
+    fan_out(send_volume)
     for d, c, copy in count_copies:
         copy.wait_send()
     for kind, d, c, copy in relay_copies:

time: 33.2 us -> 33.5 us (level)
    pallas_call x1, Pallas kernels: 31.5 us -> 31.9 us  [on_device(): pl.pallas_call(functools.partial(kernel, n_orient, n_frame), out_shape=(p...]
where the time goes in v4:
time: 33.5 us; the launch traced here: 33.4 us
  Pallas kernels  32.7 us (98%)
  between operations  0.64 us (2%)
    pallas_call x1, Pallas kernels, on_device(): pl.pallas_call(functools.partial(kernel, n_orient, n_frame), out_shape=(p...  31.9 us
    pallas_call x1, Pallas kernels, on_device(): pl.pallas_call(place, out_shape=tuple((jax.ShapeDtypeStruct(value.shape,...  0.83 us

profile of v4, /device:TPU:0, one launch (start us, length us, event | category | flops | bytes accessed | tf_op | source)
XLA Modules:
  0.0 33.4 jit_solution(5696106724385472561)
XLA Ops:
  0.6 31.9 %shard_map.76 = (bf16[128,2048]{1,0:T(8,128)(2,1)S(1)}, f32[1,24,128]{2,1,0:T(8,128)S(1)}, f32[1,256]{1,0:T(1,128)S(1)}) custom-call(bf16[128,4096]{1,0:T(8,128)(2,1)} %logt_hbm.1, s32[256,4096]{1,0:T(8,128)} %frames_hbm.1, s32[2,16,128]{2,1,0:T(8,128)} %index_hbm.1, f32[2,16,128]{2,1,0:T(8,128)} %weight_hbm.1, f32[1,24,128]{2,1,0:T(8,128)} %prior_hbm.1), custom_call_target="tpu_custom_call" | custom-call | tf_op jit(solution)/shard_map/pallas_call | solution.py:417
  32.5 0.8 %shard_map.77 = (bf16[128,2048]{1,0:T(8,128)(2,1)}, f32[1,24,128]{2,1,0:T(8,128)}, f32[1,256]{1,0:T(1,128)}) custom-call(bf16[128,2048]{1,0:T(8,128)(2,1)S(1)} %get-tuple-element.9.a_in, f32[1,24,128]{2,1,0:T(8,128)S(1)} %get-tuple-element.10.b_in, f32[1,256]{1,0:T(1,128)S(1)} %get-tuple-element.11.c_in), custom_call_target="tpu_custom_call" | custom-call | tf_op jit(solution)/shard_map/pallas_call | solution.py:470
